TPU v7x, 32 devices: a whole 2x2x4 slice. The times are simulated.
32 devices in a mesh: dp: 2 (over y), slab: 16 (over z, x, core).
Axes of the slice: x: 2, y: 2, z: 4, core: 2. Of those that a mesh axis runs over, the one named last changes fastest.
Arguments:
- profiles: float32 [2, 4, 128, 128, 128], P('dp', None, 'slab'), may hold values from -4.5 to 4.5, as said below
- target_fields: float32 [2, 2, 128, 128, 128], P('dp', None, 'slab'), may hold values from -6 to 6
- lift_weight: float32 [4, 32], replicated, may hold values from -3 to 3
- local_weight: bfloat16 [32, 32], replicated, may hold values from -1 to 1
- local_bias: float32 [32], replicated, may hold values from -4 to 4
- output_weight: bfloat16 [32, 2], replicated, may hold values from -1 to 1
- output_bias: float32 [2], replicated, may hold values from -4 to 4
- mode_weight: float32 [2, 16, 16, 16, 1024], P(None, 'slab'), may hold values from -6 to 6
Outputs:
- predicted: float32 [2, 2, 128, 128, 128], P('dp', None, 'slab')
- mode_gradient: float32 [2, 16, 16, 16, 1024], P(None, 'slab', 'dp')
Inputs may be any that keep to these rules, and one draw needn't show every extreme that they name: `profiles`: each input channel of each sample has zero mean over the grid, up to float32 rounding.
All inputs are finite; a program needn't handle non-finite values.
Results may differ from a plain program's by a relative error of at most 0.0061.
Values sent between devices are 32-bit elements; how exact they have to be, the bound alone decides.
A program may use at most 128 MiB of HBM per device.

v0:
```python
import math

import jax
import jax.numpy as jnp
from jax import lax
from jax.sharding import PartitionSpec as P

NX = 128
NY = 128
NZ = 128
KX = 16
KY = 16
KZ = 16


def mode_freqs(count):
    index_list = jnp.arange(count, dtype=jnp.int32)
    return jnp.where(index_list < count // 2, index_list, index_list - count)


def angles(positions, frequencies, length):
    product = jnp.mod(positions[:, None] * frequencies[None, :], length)
    return 2.0 * math.pi * product.astype(jnp.float32) / length


def rotation(angle_table, direction):
    cosine = jnp.cos(angle_table)
    sine_part = jnp.sin(angle_table)
    upper_row = jnp.stack([cosine, direction * sine_part], axis=-1)
    lower_row = jnp.stack([-direction * sine_part, cosine], axis=-1)
    return jnp.stack([upper_row, lower_row], axis=-2)


def forward_z():
    angle_table = angles(jnp.arange(NZ, dtype=jnp.int32), jnp.arange(KZ, dtype=jnp.int32), NZ)
    return jnp.concatenate([jnp.cos(angle_table), -jnp.sin(angle_table)], axis=1)


def inverse_z():
    angle_table = angles(jnp.arange(NZ, dtype=jnp.int32), jnp.arange(KZ, dtype=jnp.int32), NZ).T
    doubling = jnp.where(jnp.arange(KZ) == 0, 1.0, 2.0).astype(jnp.float32)[:, None]
    return jnp.concatenate(
        [doubling * jnp.cos(angle_table), -doubling * jnp.sin(angle_table)], axis=0
    )


def y_rotation(direction):
    return rotation(angles(jnp.arange(NY, dtype=jnp.int32), mode_freqs(KY), NY), direction)


def x_rotation(positions, direction):
    norm_factor = 1.0 / math.sqrt(NX * NY * NZ)
    return rotation(angles(positions, mode_freqs(KX), NX), direction) * norm_factor


def spectrum(field_in):
    highest = lax.Precision.HIGHEST
    channels, planes = (field_in.shape[0], field_in.shape[1])
    along_z = jnp.einsum("cxyz,zm->mcxy", field_in, forward_z(), precision=highest).reshape(
        2, KZ, channels, planes, NY
    )
    along_y = jnp.einsum("rkcxy,yqrs->qxskc", along_z, y_rotation(-1.0), precision=highest).reshape(
        KY, planes, 2, KZ * channels
    )
    x_table = x_rotation(
        lax.axis_index("slab") * planes + jnp.arange(planes, dtype=jnp.int32), -1.0
    )
    result = lax.psum_scatter(
        jnp.einsum("qxrm,xprs->qpsm", along_y, x_table, precision=highest),
        "slab",
        scatter_dimension=0,
        tiled=True,
    )
    return result.reshape(-1, KX, 2, KZ, channels)


def field_from(spectra):
    highest = lax.Precision.HIGHEST
    own_rows, channels = (spectra.shape[0], spectra.shape[4])
    flattened = spectra.reshape(own_rows, KX, 2, KZ * channels)
    planes = NX // lax.axis_size("slab")
    x_table = x_rotation(lax.axis_index("slab") * planes + jnp.arange(planes, dtype=jnp.int32), 1.0)
    local_part = jnp.einsum(
        "qprm,xprs->qxsm",
        lax.all_gather(flattened, "slab", axis=0, tiled=True),
        x_table,
        precision=highest,
    )
    along_y = jnp.einsum(
        "qxrkc,yqrs->skcxy",
        local_part.reshape(KY, planes, 2, KZ, channels),
        y_rotation(1.0),
        precision=highest,
    )
    result = jnp.einsum("mp,mz->pz", along_y.reshape(2 * KZ, -1), inverse_z(), precision=highest)
    return result.reshape(channels, planes, NY, NZ)


def contract(left, right):
    return jnp.einsum("qpkc,qpkco->qpko", left, right, precision=lax.Precision.HIGHEST)


def outer_product(left, right):
    return jnp.einsum("qpkc,qpko->qpkco", left, right, precision=lax.Precision.HIGHEST)


def body(
    profiles,
    target_fields,
    lift_weight,
    local_weight,
    local_bias,
    output_weight,
    output_bias,
    mode_weight,
):
    highest = lax.Precision.HIGHEST
    channels = lift_weight.shape[1]
    inputs = profiles[0]
    planes = inputs.shape[1]
    lifted = jnp.einsum("ic,ixyz->cxyz", lift_weight, inputs, precision=highest).astype(
        jnp.bfloat16
    )
    spectra = spectrum(lifted)
    own_rows = spectra.shape[0]
    weights = mode_weight.reshape(2, own_rows, KX, KZ, channels, channels)
    value_re = spectra[:, :, 0]
    value_im = spectra[:, :, 1]
    mixed_re = contract(value_re, weights[0]) - contract(value_im, weights[1])
    mixed_im = contract(value_re, weights[1]) + contract(value_im, weights[0])
    spectral = field_from(jnp.stack([mixed_re, mixed_im], axis=2))
    columns = lifted.reshape(channels, -1)
    pre_act = (
        spectral.reshape(channels, -1)
        + jnp.dot(local_weight.T, columns, preferred_element_type=jnp.float32)
        + local_bias[:, None]
    )
    activated, slope_fn = jax.vjp(lambda value: jax.nn.gelu(value, approximate=True), pre_act)
    hidden = activated.astype(jnp.bfloat16)
    predicted = (
        jnp.dot(output_weight.T, hidden, preferred_element_type=jnp.float32) + output_bias[:, None]
    )
    misfit = predicted - target_fields[0].reshape(2, -1)
    out_weights = output_weight.astype(jnp.float32)
    hidden_grad = out_weights[:, 0:1] * misfit[0:1] + out_weights[:, 1:2] * misfit[1:2]
    (pre_grad,) = slope_fn(hidden_grad)
    doubling = jnp.where(jnp.arange(KZ) == 0, 1.0, 2.0).astype(jnp.float32)
    grad_spectra = (
        spectrum(pre_grad.reshape(channels, planes, NY, NZ)) * doubling[None, None, None, :, None]
    )
    share = KX // lax.axis_size("dp")
    grad_re = grad_spectra[:, :, 0]
    grad_im = grad_spectra[:, :, 1]
    weight_re = outer_product(value_re, grad_re) + outer_product(value_im, grad_im)
    weight_im = outer_product(value_re, grad_im) - outer_product(value_im, grad_re)
    local_grads = jnp.stack([weight_re, weight_im]).reshape(
        2, own_rows, KX, KZ, channels * channels
    )
    totals = lax.psum(local_grads, "dp")
    gradients = lax.dynamic_slice_in_dim(totals, lax.axis_index("dp") * share, share, 2)
    return (predicted.reshape(1, 2, planes, NY, NZ), gradients)


def solution(mesh):
    in_specs = (
        P("dp", None, "slab", None, None),
        P("dp", None, "slab", None, None),
        P(),
        P(),
        P(),
        P(),
        P(),
        P(None, "slab", None, None, None),
    )
    out_specs = (P("dp", None, "slab", None, None), P(None, "slab", "dp", None, None))
    return jax.shard_map(body, mesh=mesh, in_specs=in_specs, out_specs=out_specs, check_vma=False)
```

profile of v0, /device:TPU:25, one launch (start us, length us, event | category | flops | bytes accessed | tf_op | source)
XLA Modules:
  0.0 540.0 jit_solution(13365860618102903291)
XLA Ops:
  8.8 15.3 %convolution_convert_fusion = bf16[32,8,128,128]{3,0,2,1:T(8,128)(2,1)S(1)} fusion(f32[4,8,128,128]{3,2,1,0:T(8,128)S(1)} %bitcast.214, f32[4,32]{1,0:T(4,128)} %param.10), kind=kOutput, calls=%fused_computation.16 | convolution fusion | flops 205520896 | bytes 10486272 | tf_op jit(solution)/shard_map/ic,ixyz->cxyz/dot_general | solution.py:121
  24.1 15.0 %fusion.40 = f32[32,32,8,128]{3,0,2,1:T(8,128)S(1)} fusion(f32[128,16]{0,1:T(8,128)S(1)} %get-tuple-element.36, f32[128,16]{0,1:T(8,128)S(1)} %get-tuple-element.37, bf16[32,8,128,128]{3,0,2,1:T(8,128)(2,1)S(1)} %convolution_convert_fusion), kind=kOutput, calls=%fused_computation.62 | convolution fusion | flops 1610616832 | bytes 12599296 | tf_op jit(solution)/shard_map/cxyz,zm->mcxy/dot_general | solution.py:59
  39.1 10.8 %fusion.20 = f32[16,8,2,16,32]{4,0,1,3,2:T(8,128)S(1)} fusion(f32[2,16,32,8,128]{4,1,0,3,2:T(8,128)S(1)} %bitcast.217, f32[128,16,1,2]{0,1,2,3:T(8,128)S(1)} %get-tuple-element.15, f32[128,16,1,2]{0,1,2,3:T(8,128)S(1)} %get-tuple-element.18), kind=kOutput, calls=%fused_computation.30 | convolution fusion | flops 402661376 | bytes 4751360 | tf_op jit(solution)/shard_map/rkcxy,yqrs->qxskc/dot_general | solution.py:62
  65.2 83.7 %all-reduce.8.cloned.1.call-done = f32[16,16,2,512]{3,1,0,2:T(8,128)} async-done(((f32[16,16,2,512]{3,1,0,2:T(8,128)}), f32[16,16,2,512]{3,1,0,2:T(8,128)}) %all-reduce.8.cloned.1.call-update) | async-done | bytes 1048592
  150.6 5.3 fusion.93
  155.9 5.2 fusion.95
  169.2 9.9 %copy.34 = bf16[32,8,128,128]{3,2,1,0:T(8,128)(2,1)} copy(bf16[32,8,128,128]{3,0,2,1:T(8,128)(2,1)} %copy-done.3) | data formatting | bytes 16777216 | tf_op jit(solution)/shard_map/convert_element_type | solution.py:121
  180.8 27.3 %all-gather.2.cloned.1.call-done = f32[16,16,2,512]{3,1,2,0:T(8,128)} async-done(((f32[1,16,2,512]{3,1,2,0:T(8,128)}), f32[16,16,2,512]{3,1,2,0:T(8,128)}) %all-gather.2.cloned.1.call-update) | async-done | bytes 1048592 | tf_op jit(solution)/shard_map/all_gather | solution.py:85
  210.5 4.1 convolution_bitcast_fusion.1
  214.6 6.2 %copy.39 = f32[2,16,32,8,128]{4,3,2,1,0:T(8,128)} copy(f32[2,16,32,8,128]{4,2,1,3,0:T(8,128)S(1)} %convolution_bitcast_fusion.1) | data formatting | bytes 8388608 | tf_op jit(solution)/shard_map/qxrkc,yqrs->skcxy/transpose | solution.py:89
  220.8 4.9 reshape.455
  225.8 29.9 %fusion.36 = f32[32768,128]{1,0:T(8,128)} fusion(f32[32,32768]{1,0:T(8,128)} %reshape.455, f32[16,128]{1,0:T(8,128)S(1)} %get-tuple-element.38, f32[16,128]{1,0:T(8,128)S(1)} %get-tuple-element.39), kind=kOutput, calls=%fused_computation.58 | convolution fusion | flops 1610616832 | bytes 20987904 | tf_op jit(solution)/shard_map/mp,mz->pz/dot_general | solution.py:95
  255.7 12.3 %reshape_reshape.3 = f32[32,131072]{1,0:T(8,128)} reshape(f32[32768,128]{1,0:T(8,128)} %fusion.36) | data formatting | bytes 33554432 | tf_op jit(solution)/shard_map/reshape;reshape | solution.py:134
  268.0 19.6 %fusion.1 = f32[32,131072]{1,0:T(8,128)} fusion(f32[32,131072]{1,0:T(8,128)} %reshape_reshape.3, bf16[32,32]{1,0:T(8,128)(2,1)S(1)} %copy-done.8, bf16[4,8,1024,128]{3,2,1,0:T(8,128)(2,1)} %bitcast.216, f32[32]{0:T(128)S(1)} %copy-done.9), kind=kOutput, calls=%fused_computation.2 | convolution fusion | flops 276824064 | bytes 41945216 | tf_op jit(solution)/shard_map/dot_general | solution.py:135
  287.6 9.9 %bitcast_subtract_fusion = (f32[2,131072]{1,0:T(2,128)S(1)}, f32[131072,2]{0,1:T(2,128)}) fusion(f32[2,131072]{1,0:T(2,128)S(1)} %copy-done.7, f32[2]{0:T(128)S(1)} %copy-done.10, bf16[32,2]{0,1:T(2,128)(2,1)S(1)} %copy-done.11, f32[32,131072]{1,0:T(8,128)} %fusion.1), kind=kOutput, calls=%fused_computation.35 | convolution fusion | flops 55050240 | bytes 19923080 | tf_op jit(solution)/shard_map/dot_general | solution.py:141
  298.5 14.1 %fusion.8 = f32[4,8,1024,128]{3,1,2,0:T(8,128)} fusion(f32[32,131072]{1,0:T(8,128)S(1)} %copy-done.2, f32[131072]{0:T(1024)S(1)} %bitcast.219, f32[32]{0:T(128)S(1)} %get-tuple-element.27, f32[131072]{0:T(1024)S(1)} %bitcast.218, f32[32]{0:T(128)S(1)} %get-tuple-element.26), kind=kLoop, calls=%fused_computation.12 | loop fusion | flops 92274688 | bytes 34603264
  312.6 9.8 %copy.70 = f32[4,8,1024,128]{3,2,1,0:T(8,128)S(1)} copy(f32[4,8,1024,128]{3,1,2,0:T(8,128)} %fusion.8) | data formatting | bytes 33554432
  322.4 17.0 %fusion.97 = f32[2,16,32,8,128]{4,1,3,2,0:T(8,128)S(1)} fusion(f32[2,16,128,1,1]{2,1,4,3,0:T(8,128)S(1)} %bitcast.230, f32[32,8,128,128,1]{3,2,1,0,4:T(8,128)S(1)} %bitcast.215), kind=kOutput, calls=%fused_computation.153 | convolution fusion | flops 1610612736 | bytes 20987904 | tf_op jit(solution)/shard_map/cxyz,zm->mcxy/dot_general | solution.py:59
  339.5 11.6 %fusion.23 = f32[16,8,2,16,32]{4,0,1,3,2:T(8,128)S(1)} fusion(f32[2,16,32,8,128]{4,1,3,2,0:T(8,128)S(1)} %fusion.97, f32[128,16,1,2]{0,1,2,3:T(8,128)S(1)} %get-tuple-element.15, f32[128,16,1,2]{0,1,2,3:T(8,128)S(1)} %get-tuple-element.18), kind=kOutput, calls=%fused_computation.31 | convolution fusion | flops 402661376 | bytes 4751360 | tf_op jit(solution)/shard_map/rkcxy,yqrs->qxskc/dot_general | solution.py:62
  358.2 90.2 %all-reduce.10.cloned.1.call-done = f32[16,16,2,512]{3,1,0,2:T(8,128)} async-done(((f32[16,16,2,512]{3,1,0,2:T(8,128)}), f32[16,16,2,512]{3,1,0,2:T(8,128)}) %all-reduce.10.cloned.1.call-update) | async-done | bytes 1048592
  450.2 4.6 multiply_add_fusion
  454.9 3.9 stack.135
  458.8 4.6 stack.136
  468.4 62.6 %all-reduce.6.cloned.1.call-done = f32[2,1,16,16,1024]{4,3,2,1,0:T(8,128)} async-done(((f32[2,1,16,16,1024]{4,3,2,1,0:T(8,128)}), f32[2,1,16,16,1024]{4,3,2,1,0:T(8,128)}) %all-reduce.6.cloned.1.call-update) | async-done | bytes 2097168 | tf_op jit(solution)/shard_map/psum | solution.py:159
  (78 shorter events, 47.8 us)
Async XLA Ops:
  7.2 1.6 copy-start
  7.2 141.7 %all-reduce.8.cloned.1.call-start = ((), (), s32[]{:S(2)}) async-start(), calls=%async_computation.2 | async-start | bytes 2097152
  24.0 25.9 %copy-start.3 = (bf16[32,8,128,128]{3,0,2,1:T(8,128)(2,1)}, bf16[32,8,128,128]{3,0,2,1:T(8,128)(2,1)S(1)}, u32[]{:S(2)}) copy-start(bf16[32,8,128,128]{3,0,2,1:T(8,128)(2,1)S(1)} %convolution_convert_fusion) | copy-start | bytes 25165828
  55.2 9.3 %copy-start.12 = (u32[32]{0:T(128)S(1)}, u32[32]{0:T(128)}, u32[]{:S(2)}) copy-start(u32[32]{0:T(128)} %constant.103) | copy-start | bytes 388
  57.2 150.9 %all-gather.2.cloned.1.call-start = ((), (), s32[]{:S(2)}) async-start(), calls=%async_computation | async-start | bytes 1114112 | tf_op jit(solution)/shard_map/all_gather | solution.py:85
  150.5 10.5 %copy-start.5 = (f32[16,16,32,32]{3,2,1,0:T(8,128)S(1)}, f32[16,16,32,32]{3,2,1,0:T(8,128)}, u32[]{:S(2)}) copy-start(f32[16,16,32,32]{3,2,1,0:T(8,128)} %reshape.453) | copy-start | bytes 3145732
  150.5 14.0 %copy-start.4 = (f32[16,16,32,32]{3,2,1,0:T(8,128)S(1)}, f32[16,16,32,32]{3,2,1,0:T(8,128)}, u32[]{:S(2)}) copy-start(f32[16,16,32,32]{3,2,1,0:T(8,128)} %reshape.451) | copy-start | bytes 3145732
  168.9 10.2 %copy-start.6 = (f32[1,2,8,128,128]{4,3,2,1,0:T(8,128)S(1)}, f32[1,2,8,128,128]{4,3,2,1,0:T(8,128)}, u32[]{:S(2)}) copy-start(f32[1,2,8,128,128]{4,3,2,1,0:T(8,128)} %param.9) | copy-start | bytes 3145732
  168.9 11.8 %copy-start.11 = (bf16[32,2]{0,1:T(2,128)(2,1)S(1)}, bf16[32,2]{0,1:T(2,128)(2,1)}, u32[]{:S(2)}) copy-start(bf16[32,2]{0,1:T(2,128)(2,1)} %param.13) | copy-start | bytes 388
  168.9 279.5 %all-reduce.10.cloned.1.call-start = ((), (), s32[]{:S(2)}) async-start(), calls=%async_computation.3 | async-start | bytes 2097152
  255.7 12.3 %copy-start.8 = (bf16[32,32]{1,0:T(8,128)(2,1)S(1)}, bf16[32,32]{1,0:T(8,128)(2,1)}, u32[]{:S(2)}) copy-start(bf16[32,32]{1,0:T(8,128)(2,1)} %param.11) | copy-start | bytes 6148
  255.7 12.3 %copy-start.9 = (f32[32]{0:T(128)S(1)}, f32[32]{0:T(128)}, u32[]{:S(2)}) copy-start(f32[32]{0:T(128)} %param.12) | copy-start | bytes 388
  268.0 19.6 %copy-start.7 = (f32[2,131072]{1,0:T(2,128)S(1)}, f32[2,131072]{1,0:T(2,128)}, u32[]{:S(2)}) copy-start(f32[2,131072]{1,0:T(2,128)} %reshape_squeeze.3) | copy-start | bytes 3145732
  268.0 19.6 %copy-start.10 = (f32[2]{0:T(128)S(1)}, f32[2]{0:T(128)}, u32[]{:S(2)}) copy-start(f32[2]{0:T(128)} %param.14) | copy-start | bytes 28
  287.6 10.9 %copy-start.2 = (f32[32,131072]{1,0:T(8,128)S(1)}, f32[32,131072]{1,0:T(8,128)}, u32[]{:S(2)}) copy-start(f32[32,131072]{1,0:T(8,128)} %fusion.1) | copy-start | bytes 50331652
  358.1 172.8 %all-reduce.6.cloned.1.call-start = ((), (), s32[]{:S(2)}) async-start(), calls=%async_computation.1 | async-start | bytes 4194304 | tf_op jit(solution)/shard_map/psum | solution.py:159
  454.9 78.4 %copy-start.1 = (f32[1,4,8,128,128]{4,3,2,1,0:T(8,128)S(1)}, f32[1,4,8,128,128]{4,3,2,1,0:T(8,128)}, u32[]{:S(2)}) copy-start(f32[1,4,8,128,128]{4,3,2,1,0:T(8,128)} %param.8) | copy-start | bytes 6291460
Sparse Core Ops, SparseCore 0:
  57.3 91.4 all-reduce.7
  169.0 39.0 all-gather.1
  358.3 90.1 all-reduce.9
  466.2 64.6 all-reduce.5
where the time goes:
time: 546 us; the launch traced here: 540 us
  waiting for transfers between devices  264 us (48%)
  matrix products  156 us (29%)
  local copies, waits for them, and re-layouts  82.3 us (15%)
  other arithmetic  22.6 us (4%)
  between operations  14.4 us (3%)
    unnamed x6, waiting for transfers between devices  174 us
    psum x1, waiting for transfers between devices, body(): totals = lax.psum(local_grads, 'dp')  62.6 us
    dot_general x2, matrix products, spectrum(): jnp.einsum('cxyz,zm->mcxy', field_in, forward_z(), precision=highest)  32.1 us
    dot_general x1, matrix products, field_from(): jnp.einsum('mp,mz->pz', along_y.reshape(2 * KZ, -1), inverse_z(), precisi...  29.9 us
    all_gather x1, waiting for transfers between devices, field_from(): lax.all_gather(flattened, 'slab', axis=0, tiled=True)  27.3 us
    dot_general x2, matrix products, spectrum(): jnp.einsum('rkcxy,yqrs->qxskc', along_z, y_rotation(-1.0), precision=high...  22.4 us
    dot_general x1, matrix products, body(): jnp.dot(local_weight.T, columns, preferred_element_type=jnp.float32)  19.6 us
    unnamed x31, local copies, waits for them, and re-layouts  17.4 us
  transfers between devices with their start and end apart: 4, of which 4 were waited for; matrix products, arithmetic and copies ran while one was open for 4% of the time, Pallas kernels for 0%

commit v1 on v0

v1 whole, which is shorter than its diff:
```python
import functools
import math

import jax
import jax.numpy as jnp
import ml_dtypes
import numpy as np
from jax import lax
from jax.experimental import pallas as pl
from jax.experimental.pallas import tpu as pltpu
from jax.sharding import PartitionSpec as P

N = 128
K = 16
C = 32
NIN = 4
MESH = pl.DeviceIdType.MESH
BF = jnp.bfloat16
F32 = jnp.float32


def halves(table):
    table = np.asarray(table, np.float32)
    high = table.astype(ml_dtypes.bfloat16)
    low = (table - high.astype(np.float32)).astype(ml_dtypes.bfloat16)
    return high, low


def tables():
    freq = np.where(np.arange(K) < K // 2, np.arange(K), np.arange(K) - K)
    cell = np.arange(N)
    signed = 2.0 * np.pi * np.mod(freq[:, None] * cell[None, :], N) / N
    plain = 2.0 * np.pi * np.mod(np.arange(K)[:, None] * cell[None, :], N) / N
    norm = 1.0 / math.sqrt(N * N * N)
    doubling = np.where(np.arange(K) == 0, 1.0, 2.0)
    fy = np.concatenate([np.cos(signed), -np.sin(signed)], axis=0)
    fy_h, fy_l = halves(fy)
    fy_pair = np.concatenate([fy_h, fy_l], axis=0)
    zc, zs = np.cos(plain).T, np.sin(plain).T

    def place(count):
        out = np.zeros((count, 2, N, 2, count, K))
        for c in range(count):
            out[c, 0, :, 0, c], out[c, 0, :, 1, c] = zc, -zs
            out[c, 1, :, 0, c], out[c, 1, :, 1, c] = zs, zc
        return out.reshape(count * 2 * N, 2 * count * K)

    back = np.zeros((2, 8, K, 8, 2, N))
    for c in range(8):
        wc, ws = doubling[:, None] * np.cos(plain), doubling[:, None] * np.sin(plain)
        back[0, c, :, c, 0], back[0, c, :, c, 1] = wc, ws
        back[1, c, :, c, 0], back[1, c, :, c, 1] = -ws, wc
    back = back.reshape(2 * 8 * K, 8 * 2 * N)
    iy_h, iy_l = halves(np.concatenate([np.cos(signed).T, -np.sin(signed).T], axis=1))
    iy = np.concatenate([iy_h, iy_h, iy_l], axis=1)
    fx = np.concatenate([np.cos(signed), -np.sin(signed)], axis=0) * norm
    ix = np.stack([np.repeat(np.cos(signed).T, K, axis=1), np.repeat(np.sin(signed).T, K, axis=1)]) * norm
    rep = np.zeros((4, C, C, K))
    for c in range(C):
        rep[0, c, c, :] = 1.0
    rep = rep.reshape(4 * C, C * K).astype(ml_dtypes.bfloat16)
    tile = np.zeros((C, K, 4, C))
    for c in range(C):
        tile[c, :, :, c] = 1.0
    tile = tile.reshape(C * K, 4 * C).astype(ml_dtypes.bfloat16)
    hit = (np.arange(N)[None, :] % K == np.arange(K)[:, None]).astype(np.float32)
    first = (np.arange(N) < N // 2).astype(np.float32)
    corner = np.zeros((K, N))
    corner[0, N // 2 : N // 2 + C] = 1.0
    owner = np.zeros((N, C, C))
    for c in range(C):
        owner[N // 2 + c, c, :] = 1.0
    owner = owner.reshape(N, C * C).astype(ml_dtypes.bfloat16)
    masks = np.stack([hit, hit * first, hit * (1 - first), np.broadcast_to(np.tile(doubling, 8), (K, N)), np.broadcast_to(1.0 - 2.0 * first, (K, N)), corner]).astype(np.float32)
    return [fy_pair, *halves(place(NIN)), *halves(place(8)), *halves(back), iy, *halves(fx), *halves(ix), rep, tile, owner, masks]


def split(value):
    high = value.astype(BF)
    return high, (value - high.astype(F32)).astype(BF)


def mm(left, right):
    return jnp.dot(left, right, preferred_element_type=F32)


def left3(value, high, low):
    a, b = split(value)
    return mm(a, high) + mm(b, high) + mm(a, low)


def right3(high, low, value):
    a, b = split(value)
    return mm(high, a) + mm(high, b) + mm(low, a)


def kernel(dp, slab, prof, targ, modes, lift_wide, lift, local, bias, outw, outb,
           fy, zp_h, zp_l, zg_h, zg_l, iz_h, iz_l, iy, fx_h, fx_l, ix_h, ix_l, rep, tile, owner, masks,
           pred, grad,
           ubuf, resid, rows_pad, sp, rp, spec, e_h, e_l, wide, s_re, s_im, mixed, sm, rm, pm, b_h, b_l,
           field, slope, acc, sg, rg, xs, rx, g_re, g_im,
           p_send, p_recv, m_send, m_recv, g_send, g_recv, x_send, x_recv):
    me = lax.axis_index("slab")
    mine = lax.axis_index("dp")
    planes = prof.shape[1]
    share = K // dp

    barrier = pltpu.get_barrier_semaphore()
    for step in range(1, slab):
        pl.semaphore_signal(barrier, inc=1, device_id={"slab": lax.rem(me + step, slab)}, device_id_type=MESH)
    for step in range(1, dp):
        pl.semaphore_signal(barrier, inc=1, device_id={"dp": lax.rem(mine + step, dp)}, device_id_type=MESH)

    def copies(source, target, send, recv, axis, here, count):
        out = []
        for step in range(1, count):
            peer = lax.rem(here + step, count)
            origin = lax.rem(here + count - step, count)
            going = pltpu.make_async_remote_copy(
                src_ref=source.at[peer], dst_ref=target.at[here], send_sem=send.at[peer], recv_sem=recv.at[here],
                device_id={axis: peer}, device_id_type=MESH)
            coming = pltpu.make_async_remote_copy(
                src_ref=source.at[peer], dst_ref=target.at[origin], send_sem=send.at[peer], recv_sem=recv.at[origin],
                device_id={axis: peer}, device_id_type=MESH)
            out.append((going, coming))
        return out

    def launch(pairs, source, target, here):
        for going, _ in pairs:
            going.start()
        target[pl.ds(here, 1)] = source[pl.ds(here, 1)]

    def finish(pairs):
        for going, coming in pairs:
            coming.wait_recv()
        for going, _ in pairs:
            going.wait_send()

    e_h[...] = owner[...]
    e_l[...] = jnp.zeros_like(e_l)
    for i in range(NIN):
        e_row = lift_wide[i : i + 1, :]
        high, low = split(jnp.broadcast_to(e_row, (K, C * C)))
        e_h[i * K : (i + 1) * K, :] = high
        e_l[i * K : (i + 1) * K, :] = low
    resid[...] = jnp.zeros_like(resid)

    @pl.loop(0, planes)
    def _(x):
        rows = pl.ds(pl.multiple_of(x * K, K), K)
        for i in range(NIN):
            high, low = split(prof[i, x])
            both = mm(fy[...], high)
            u = both[: 2 * K] + both[2 * K :] + mm(fy[: 2 * K, :], low)
            ubuf[rows, 2 * i * N : (2 * i + 1) * N] = u[:K]
            ubuf[rows, (2 * i + 1) * N : (2 * i + 2) * N] = u[K:]

        @pl.loop(0, C // 4)
        def _(group):
            totals = [resid[group * 4 + j] for j in range(4)]
            for chunk in range(4):
                ys = slice(chunk * 32, (chunk + 1) * 32)
                inputs = [prof[i, x, ys, :] for i in range(NIN)]
                for j in range(4):
                    c = group * 4 + j
                    value = lift[0, c] * inputs[0]
                    for i in range(1, NIN):
                        value = value + lift[i, c] * inputs[i]
                    lost = value.astype(BF).astype(F32) - value
                    totals[j] = totals[j] + jnp.sum(lost.reshape(4, 8, N), axis=0)
            for j in range(4):
                resid[group * 4 + j] = totals[j]

    v = left3(ubuf[:, : 2 * NIN * N], zp_h[...], zp_l[...])
    for x in range(planes):
        sp[:, x, :N] = v[x * K : (x + 1) * K, :]
    rows_pad[...] = jnp.zeros_like(rows_pad)
    rows_pad[N // 2 : N // 2 + C, :] = jnp.sum(resid[...], axis=1)
    high, low = split(rows_pad[...])
    ones = jnp.ones((planes, N), BF)
    dims = (((1,), (1,)), ((), ()))
    sums = lax.dot_general(ones, high, dims, preferred_element_type=F32)
    sums = sums + lax.dot_general(ones, low, dims, preferred_element_type=F32)
    for q in range(slab):
        sp[q, :, N:] = sums

    pl.semaphore_wait(barrier, slab + dp - 2)
    pairs = copies(sp, rp, p_send, p_recv, "slab", me, slab)
    launch(pairs, sp, rp, me)
    finish(pairs)

    y = right3(fx_h[...], fx_l[...], rp[:, :, :N].reshape(N, N))
    spec[:, :N] = y[:K] + masks[4] * pltpu.roll(y[K:], N // 2, 1)
    sums = jnp.sum(rp[:, :, N:].reshape(N, N), axis=0, keepdims=True)
    scale = jnp.where(me == 0, 1.0 / (planes * math.sqrt(N * N * N)), 0.0).astype(F32)
    spec[:, N:] = jnp.zeros((K, N), F32)
    spec[:1, N:] = sums * scale

    def expand(row_of, count):
        for p in range(count):
            row, lost = row_of(p)
            row = jnp.broadcast_to(row, (K, N))
            wide[0, p * K : (p + 1) * K, :] = row * masks[1] + jnp.broadcast_to(lost, (K, N)) * masks[5]
            wide[1, p * K : (p + 1) * K, :] = pltpu.roll(row * masks[2], N // 2, 1)
        used = count * K
        s_re[:used, :] = left3(wide[0, :used, :], e_h[...], e_l[...])
        s_im[:used, :] = left3(wide[1, :used, :], e_h[...], e_l[...])

    expand(lambda p: (spec[p : p + 1, :N], spec[p : p + 1, N:]), K)

    @pl.loop(0, K * K // 16)
    def _(block):
        rows = pl.ds(pl.multiple_of(block * 16, 16), 16)
        total_re = jnp.zeros((16, N), F32)
        total_im = jnp.zeros((16, N), F32)
        for t in range(C * C // N):
            lanes = slice(t * N, (t + 1) * N)
            a, b, c, d = s_re[rows, lanes], s_im[rows, lanes], modes[0, rows, lanes], modes[1, rows, lanes]
            total_re += a * c - b * d
            total_im += a * d + b * c
        for part, value in enumerate((total_re, total_im)):
            value = value + pltpu.roll(value, 64, 1)
            mixed[part, rows, :] = value + pltpu.roll(value, 32, 1)

    spread = []
    for part in range(2):
        high, low = split(mixed[part])
        spread.append((mm(high, rep[...]) + mm(low, rep[...])))
    for og in range(4):
        lanes = slice(og * N, (og + 1) * N)
        keep = jnp.broadcast_to(masks[0][None], (K, K, N)).reshape(K * K, N)
        re, im = spread[0][:, lanes] * keep, spread[1][:, lanes] * keep
        out_re = right3(ix_h[0], ix_l[0], re) - right3(ix_h[1], ix_l[1], im)
        out_im = right3(ix_h[0], ix_l[0], im) + right3(ix_h[1], ix_l[1], re)
        sm[:, :, 2 * og * N : (2 * og + 1) * N] = out_re.reshape(slab, planes, N)
        sm[:, :, (2 * og + 1) * N : (2 * og + 2) * N] = out_im.reshape(slab, planes, N)

    pairs = copies(sm, rm, m_send, m_recv, "slab", me, slab)
    launch(pairs, sm, rm, me)
    finish(pairs)

    for x in range(planes):
        pm[x * K : (x + 1) * K, :] = rm[:, x, :]
    for og in range(4):
        high, low = split(pm[:, og * 2 * N : (og + 1) * 2 * N])

        for t in range(8):
            lanes = slice(t * 2 * N, (t + 1) * 2 * N)
            value = mm(high, iz_h[:, lanes]) + mm(low, iz_h[:, lanes]) + mm(high, iz_l[:, lanes])
            v_h, v_l = split(value)
            b_h[og * 8 + t] = v_h
            b_l[og * 8 + t] = v_l

    c0 = math.sqrt(2.0 / math.pi)
    c1 = c0 * 0.044715

    @pl.loop(0, planes)
    def _(x):
        rows = pl.ds(pl.multiple_of(x * K, K), K)
        acc[...] = jnp.zeros_like(acc)

        @pl.loop(0, C // 2)
        def _(pair):
            blocks = []
            for half in range(2):
                o = pair * 2 + half
                h = b_h[o, rows, :]
                l = b_l[o, rows, :]
                blocks.append(jnp.concatenate([h[:, :N], h[:, N:], l[:, :N], l[:, N:], h[:, :N], h[:, N:]], axis=0))
            field[...] = mm(iy[...], jnp.concatenate(blocks, axis=1))
            for chunk in range(4):
                ys = slice(chunk * 32, (chunk + 1) * 32)
                inputs = [prof[i, x, ys, :] for i in range(NIN)]
                add0, add1 = acc[0, ys, :], acc[1, ys, :]
                for half in range(2):
                    o = pair * 2 + half
                    v = field[ys, half * N : (half + 1) * N] + bias[o]
                    for i in range(NIN):
                        v = v + local[i, o] * inputs[i]
                    sq = v * v
                    t = jnp.tanh(v * (c0 + c1 * sq))
                    up = 0.5 + 0.5 * t
                    hidden = (v * up).astype(BF).astype(F32)
                    slope[o, ys, :] = up + (0.5 * v) * (1.0 - t * t) * (c0 + (3.0 * c1) * sq)
                    add0 = add0 + outw[o, 0] * hidden
                    add1 = add1 + outw[o, 1] * hidden
                acc[0, ys, :] = add0
                acc[1, ys, :] = add1

        for j in range(2):
            value = acc[j] + outb[j]
            pred[j, x] = value
            acc[j] = value - targ[j, x]

        @pl.loop(0, C // 2)
        def _(pair):
            parts = []
            for half in range(2):
                o = pair * 2 + half
                parts.append(((outw[o, 0] * acc[0] + outw[o, 1] * acc[1]) * slope[o]).astype(BF))
            both = mm(fy[...], jnp.concatenate(parts, axis=1))
            u = both[: 2 * K] + both[2 * K :]
            at = pl.multiple_of(pair * 4 * N, 4 * N)
            for half in range(2):
                lanes = slice(half * N, (half + 1) * N)
                ubuf[rows, pl.ds(at + 2 * half * N, N)] = u[:K, lanes]
                ubuf[rows, pl.ds(at + (2 * half + 1) * N, N)] = u[K:, lanes]

    for og in range(4):
        v = left3(ubuf[:, og * 16 * N : (og + 1) * 16 * N], zg_h[...], zg_l[...])
        for x in range(planes):
            sg[:, x, og * 2 * N : (og + 1) * 2 * N] = v[x * K : (x + 1) * K, :]

    pairs = copies(sg, rg, g_send, g_recv, "slab", me, slab)
    launch(pairs, sg, rg, me)
    finish(pairs)

    y = right3(fx_h[...], fx_l[...], rg[...].reshape(N, 8 * N))
    for og in range(4):
        re, im = slice(2 * og * N, (2 * og + 1) * N), slice((2 * og + 1) * N, (2 * og + 2) * N)
        out_re = (y[:K, re] - y[K:, im]) * masks[3]
        out_im = (y[:K, im] + y[K:, re]) * masks[3]
        for d in range(dp):
            ps = slice(d * share, (d + 1) * share)
            xs[d, :, re] = out_re[ps]
            xs[d, :, im] = out_im[ps]
    for d in range(dp):
        xs[d, :, 8 * N : 10 * N] = spec[d * share : (d + 1) * share, :]

    pairs = copies(xs, rx, x_send, x_recv, "dp", mine, dp)
    launch(pairs, xs, rx, mine)
    finish(pairs)

    used = share * K
    for d in range(dp):
        expand(lambda p: (rx[d, p : p + 1, 8 * N : 9 * N], rx[d, p : p + 1, 9 * N : 10 * N]), share)
        for part, out in enumerate((g_re, g_im)):
            total = None
            for og in range(4):
                lanes = slice((2 * og + part) * N, (2 * og + part + 1) * N)
                for p in range(share):
                    row = jnp.broadcast_to(rx[d, p : p + 1, lanes], (K, N))
                    wide[0, p * K : (p + 1) * K, :] = row * masks[0]
                high, low = split(wide[0, :used, :])
                term = tile[og * N : (og + 1) * N, :]
                value = mm(high, term) + mm(low, term)
                total = value if total is None else total + value
            out[...] = total
        for t in range(C * C // N):
            lanes = slice(t * N, (t + 1) * N)
            a, b = s_re[:used, lanes], s_im[:used, lanes]
            w_re = a * g_re[...] + b * g_im[...]
            w_im = a * g_im[...] - b * g_re[...]
            if d == 0:
                grad[0, :, lanes] = w_re
                grad[1, :, lanes] = w_im
            else:
                grad[0, :, lanes] += w_re
                grad[1, :, lanes] += w_im


def body(dp, slab, consts, profiles, target_fields, lift_weight, local_weight, local_bias, output_weight, output_bias, mode_weight):
    planes = profiles.shape[2]
    share = K // dp
    local = jnp.sum(lift_weight[:, :, None] * local_weight.astype(F32)[None], axis=1)
    lift_wide = jnp.repeat(lift_weight, C, axis=1)
    vmem = pl.BlockSpec(memory_space=pltpu.VMEM)
    smem = pl.BlockSpec(memory_space=pltpu.SMEM)
    dma = pltpu.SemaphoreType.DMA
    pred, grad = pl.pallas_call(
        functools.partial(kernel, dp, slab),
        out_shape=(jax.ShapeDtypeStruct((2, planes, N, N), F32), jax.ShapeDtypeStruct((2, share * K, C * C), F32)),
        in_specs=[vmem] * 4 + [smem] * 5 + [vmem] * len(consts),
        out_specs=(vmem, vmem),
        scratch_shapes=[
            pltpu.VMEM((planes * K, C * 2 * N), F32),
            pltpu.VMEM((C, 8, N), F32),
            pltpu.VMEM((N, N), F32),
            pltpu.VMEM((slab, planes, 2 * N), F32),
            pltpu.VMEM((slab, planes, 2 * N), F32),
            pltpu.VMEM((K, 2 * N), F32),
            pltpu.VMEM((N, C * C), BF),
            pltpu.VMEM((N, C * C), BF),
            pltpu.VMEM((2, K * K, N), F32),
            pltpu.VMEM((K * K, C * C), F32),
            pltpu.VMEM((K * K, C * C), F32),
            pltpu.VMEM((2, K * K, N), F32),
            pltpu.VMEM((slab, planes, 8 * N), F32),
            pltpu.VMEM((slab, planes, 8 * N), F32),
            pltpu.VMEM((planes * K, 8 * N), F32),
            pltpu.VMEM((C, planes * K, 2 * N), BF),
            pltpu.VMEM((C, planes * K, 2 * N), BF),
            pltpu.VMEM((N, 2 * N), F32),
            pltpu.VMEM((C, N, N), F32),
            pltpu.VMEM((2, N, N), F32),
            pltpu.VMEM((slab, planes, 8 * N), F32),
            pltpu.VMEM((slab, planes, 8 * N), F32),
            pltpu.VMEM((dp, share, 10 * N), F32),
            pltpu.VMEM((dp, share, 10 * N), F32),
            pltpu.VMEM((share * K, N), F32),
            pltpu.VMEM((share * K, N), F32),
            dma((slab,)), dma((slab,)), dma((slab,)), dma((slab,)), dma((slab,)), dma((slab,)), dma((dp,)), dma((dp,)),
        ],
        compiler_params=pltpu.CompilerParams(collective_id=0, has_side_effects=True, vmem_limit_bytes=56 << 20),
    )(profiles[0], target_fields[0], mode_weight.reshape(2, K * K, C * C), lift_wide, lift_weight, local, local_bias,
      output_weight.astype(F32), output_bias, *consts)
    return pred[None], grad.reshape(2, 1, share, K, C * C)


def solution(mesh):
    consts = tables()
    in_specs = (
        P("dp", None, "slab", None, None),
        P("dp", None, "slab", None, None),
        P(),
        P(),
        P(),
        P(),
        P(),
        P(None, "slab", None, None, None),
    )
    out_specs = (P("dp", None, "slab", None, None), P(None, "slab", "dp", None, None))

    def run(*args):
        return body(mesh.shape["dp"], mesh.shape["slab"], [jnp.asarray(c) for c in consts], *args)

    return jax.shard_map(run, mesh=mesh, in_specs=in_specs, out_specs=out_specs, check_vma=False)
```

time: 546 us -> 122 us (0.22); the launches traced: 540 us -> 122 us
  waiting for transfers between devices: 264 us -> 0 us
  matrix products: 156 us -> 0 us
  Pallas kernels: 0 us -> 113 us
  local copies, waits for them, and re-layouts: 82.3 us -> 6.17 us
  other arithmetic: 22.6 us -> 2.07 us
  between operations: 14.4 us -> 0.65 us
    unnamed x6 -> x0, waiting for transfers between devices: 174 us -> none
    dot_general x16 -> x0, matrix products: 156 us -> none  [the longest x2 32.1 us: spectrum(): jnp.einsum('cxyz,zm->mcxy', field_in, forward_z(), precision=highest)]
    pallas_call x0 -> x1, Pallas kernels: none -> 113 us  [body(): pl.pallas_call(functools.partial(kernel, dp, slab), out_shape=(jax.ShapeD...]
    psum x1 -> x0, waiting for transfers between devices: 62.6 us -> none  [body(): totals = lax.psum(local_grads, 'dp')]
    another operation x10 -> x0, local copies, waits for them, and re-layouts: 28.1 us -> none  [the longest x1 12.3 us: body(): spectral.reshape(channels, -1)]
    all_gather x1 -> x0, waiting for transfers between devices: 27.3 us -> none  [field_from(): lax.all_gather(flattened, 'slab', axis=0, tiled=True)]
    unnamed x1 -> x0, other arithmetic: 14.1 us -> none
    unnamed x31 -> x4, local copies, waits for them, and re-layouts: 17.4 us -> 3.36 us
  transfers between devices with their start and end apart: 4 -> 0, of which waited for: 4 -> 0; matrix products, arithmetic and copies ran while one was open for 4% -> 0% of each run, Pallas kernels for 0% -> 0%
where the time goes in v1:
time: 122 us
  Pallas kernels  113 us (93%)
  local copies, waits for them, and re-layouts  6.17 us (5%)
  other arithmetic  2.07 us (2%)
    pallas_call x1, Pallas kernels, body(): pl.pallas_call(functools.partial(kernel, dp, slab), out_shape=(jax.ShapeD...  113 us
    unnamed x4, local copies, waits for them, and re-layouts  3.36 us

profile of v1, /device:TPU:25, one launch (start us, length us, event | category | flops | bytes accessed | tf_op | source)
XLA Modules:
  0.0 121.9 jit_solution(6726424903150965243)
XLA Ops:
  0.6 0.7 convert_element_type.6
  1.3 1.4 %multiply_reduce_fusion.local = f32[4,32]{1,0:T(4,128)} fusion(f32[32,32]{1,0:T(8,128)S(1)} %convert_element_type.6, f32[4,32]{1,0:T(4,128)} %lift.1), kind=kLoop, calls=%fused_computation | loop fusion | flops 8064 | bytes 5120 | tf_op jit(solution)/shard_map/reduce_sum | solution.py:365
  2.7 1.3 %copy.28.outw = f32[32,2]{1,0:T(8,128)} copy(bf16[32,2]{0,1:T(2,128)(2,1)} %param.29) | data formatting | bytes 384 | tf_op jit(solution)/shard_map/convert_element_type | solution.py:406
  4.1 0.8 broadcast_in_dim.8
  4.8 0.7 reshape.16.lift_wide
  5.5 113.0 %shard_map.239 = (f32[2,8,128,128]{3,2,1,0:T(8,128)}, f32[2,128,1024]{2,1,0:T(8,128)}) custom-call(f32[4,8,128,128]{3,2,1,0:T(8,128)} %bitcast.7, f32[2,8,128,128]{3,2,1,0:T(8,128)} %bitcast.11, f32[2,256,1024]{2,1,0:T(8,128)} %bitcast.8, f32[4,1024]{1,0:T(4,128)} %reshape.16.lift_wide, f32[4,32]{1,0:T(4,128)} %lift.1, f32[4,32]{1,0:T(4,128)} %multiply_reduce_fusion.local, ...), custom_call_target="tpu_custom_call" | custom-call | tf_op jit(solution)/shard_map/pallas_call | solution.py:370
  118.5 0.0 copy-start
  118.5 2.4 %copy.32 = f32[1,2,8,128,128]{4,3,2,1,0:T(8,128)} copy(f32[1,2,8,128,128]{4,3,2,1,0:T(8,128)} %bitcast.10) | data formatting | bytes 2097152
  120.9 0.0 copy-done
  120.9 1.0 copy.33
Async XLA Ops:
  118.5 2.4 %copy-start = (f32[2,128,1024]{2,1,0:T(8,128)S(1)}, f32[2,128,1024]{2,1,0:T(8,128)}, u32[]{:S(2)}) copy-start(f32[2,128,1024]{2,1,0:T(8,128)} %get-tuple-element.5) | copy-start | bytes 3145732

commit v2 on v1

--- a/solution.py
+++ b/solution.py
@@ -51,8 +51,7 @@
         back[0, c, :, c, 0], back[0, c, :, c, 1] = wc, ws
         back[1, c, :, c, 0], back[1, c, :, c, 1] = -ws, wc
     back = back.reshape(2 * 8 * K, 8 * 2 * N)
-    iy_h, iy_l = halves(np.concatenate([np.cos(signed).T, -np.sin(signed).T], axis=1))
-    iy = np.concatenate([iy_h, iy_h, iy_l], axis=1)
+    iy_h, _ = halves(np.concatenate([np.cos(signed).T, -np.sin(signed).T], axis=1))
     fx = np.concatenate([np.cos(signed), -np.sin(signed)], axis=0) * norm
     ix = np.stack([np.repeat(np.cos(signed).T, K, axis=1), np.repeat(np.sin(signed).T, K, axis=1)]) * norm
     rep = np.zeros((4, C, C, K))
@@ -72,7 +71,7 @@
         owner[N // 2 + c, c, :] = 1.0
     owner = owner.reshape(N, C * C).astype(ml_dtypes.bfloat16)
     masks = np.stack([hit, hit * first, hit * (1 - first), np.broadcast_to(np.tile(doubling, 8), (K, N)), np.broadcast_to(1.0 - 2.0 * first, (K, N)), corner]).astype(np.float32)
-    return [fy_pair, *halves(place(NIN)), *halves(place(8)), *halves(back), iy, *halves(fx), *halves(ix), rep, tile, owner, masks]
+    return [fy_pair, *halves(place(NIN)), halves(place(8))[0], halves(back)[0], iy_h, *halves(fx), *halves(ix), rep, tile, owner, masks]
 
 
 def split(value):
@@ -94,11 +93,11 @@
     return mm(high, a) + mm(high, b) + mm(low, a)
 
 
-def kernel(dp, slab, prof, targ, modes, lift_wide, lift, local, bias, outw, outb,
-           fy, zp_h, zp_l, zg_h, zg_l, iz_h, iz_l, iy, fx_h, fx_l, ix_h, ix_l, rep, tile, owner, masks,
+def kernel(dp, slab, prof, targ, modes, lift_rows, local, outw_rows, lift, bias, outb,
+           fy, zp_h, zp_l, zg, iz, iy, fx_h, fx_l, ix_h, ix_l, rep, tile, owner, masks,
            pred, grad,
-           ubuf, resid, rows_pad, sp, rp, spec, e_h, e_l, wide, s_re, s_im, mixed, sm, rm, pm, b_h, b_l,
-           field, slope, acc, sg, rg, xs, rx, g_re, g_im,
+           ubuf, resid, rows_pad, sp, rp, spec, e_h, e_l, wide, s_re, s_im, mixed, sm, rm, pm, b_h,
+           field_a, field_b, pre, mix, outw, acc, sg, rg, xs, rx, g_re, g_im,
            p_send, p_recv, m_send, m_recv, g_send, g_recv, x_send, x_recv):
     me = lax.axis_index("slab")
     mine = lax.axis_index("dp")
@@ -138,11 +137,21 @@
 
     e_h[...] = owner[...]
     e_l[...] = jnp.zeros_like(e_l)
+    eye = lax.broadcasted_iota(jnp.int32, (C, C), 0) == lax.broadcasted_iota(jnp.int32, (C, C), 1)
+
+    def down(row):
+        high, low = split(jnp.where(eye, jnp.broadcast_to(row, (C, C)), 0.0))
+        ones = jnp.ones((C, N), BF)
+        return mm(high, ones) + mm(low, ones)
+
     for i in range(NIN):
-        e_row = lift_wide[i : i + 1, :]
-        high, low = split(jnp.broadcast_to(e_row, (K, C * C)))
-        e_h[i * K : (i + 1) * K, :] = high
-        e_l[i * K : (i + 1) * K, :] = low
+        high, low = split(jnp.broadcast_to(lift_rows[i : i + 1, :], (K, C)))
+        pick = owner[N // 2 : N // 2 + C, :]
+        e_h[i * K : (i + 1) * K, :] = mm(high, pick).astype(BF)
+        e_l[i * K : (i + 1) * K, :] = mm(low, pick).astype(BF)
+        mix[i] = down((mm(high, local[...]) + mm(low, local[...]))[:1, :])
+    for j in range(2):
+        outw[j] = down(outw_rows[...].astype(F32)[j : j + 1, :])
     resid[...] = jnp.zeros_like(resid)
 
     @pl.loop(0, planes)
@@ -237,19 +246,29 @@
 
     pairs = copies(sm, rm, m_send, m_recv, "slab", me, slab)
     launch(pairs, sm, rm, me)
+
+    @pl.loop(0, planes)
+    def _(x):
+        @pl.loop(0, C // 4)
+        def _(group):
+            for chunk in range(4):
+                ys = slice(chunk * 32, (chunk + 1) * 32)
+                inputs = [prof[i, x, ys, :] for i in range(NIN)]
+                for j in range(4):
+                    o = group * 4 + j
+                    value = mix[0, pl.ds(o, 1), :] * inputs[0] + bias[o]
+                    for i in range(1, NIN):
+                        value = value + mix[i, pl.ds(o, 1), :] * inputs[i]
+                    pre[x, o, ys, :] = value
+
     finish(pairs)
 
     for x in range(planes):
         pm[x * K : (x + 1) * K, :] = rm[:, x, :]
     for og in range(4):
-        high, low = split(pm[:, og * 2 * N : (og + 1) * 2 * N])
-
+        high = pm[:, og * 2 * N : (og + 1) * 2 * N].astype(BF)
         for t in range(8):
-            lanes = slice(t * 2 * N, (t + 1) * 2 * N)
-            value = mm(high, iz_h[:, lanes]) + mm(low, iz_h[:, lanes]) + mm(high, iz_l[:, lanes])
-            v_h, v_l = split(value)
-            b_h[og * 8 + t] = v_h
-            b_l[og * 8 + t] = v_l
+            b_h[og * 8 + t] = mm(high, iz[:, t * 2 * N : (t + 1) * 2 * N]).astype(BF)
 
     c0 = math.sqrt(2.0 / math.pi)
     c1 = c0 * 0.044715
@@ -259,55 +278,64 @@
         rows = pl.ds(pl.multiple_of(x * K, K), K)
         acc[...] = jnp.zeros_like(acc)
 
-        @pl.loop(0, C // 2)
-        def _(pair):
+        def lines(pair):
             blocks = []
             for half in range(2):
-                o = pair * 2 + half
-                h = b_h[o, rows, :]
-                l = b_l[o, rows, :]
-                blocks.append(jnp.concatenate([h[:, :N], h[:, N:], l[:, :N], l[:, N:], h[:, :N], h[:, N:]], axis=0))
-            field[...] = mm(iy[...], jnp.concatenate(blocks, axis=1))
+                b = b_h[pair * 2 + half, rows, :]
+                blocks.append(jnp.concatenate([b[:, :N], b[:, N:]], axis=0))
+            return mm(iy[...], jnp.concatenate(blocks, axis=1))
+
+        def activate(field, pair):
+            w = [[outw[j, pl.ds(pair * 2 + half, 1), :] for j in range(2)] for half in range(2)]
             for chunk in range(4):
                 ys = slice(chunk * 32, (chunk + 1) * 32)
-                inputs = [prof[i, x, ys, :] for i in range(NIN)]
                 add0, add1 = acc[0, ys, :], acc[1, ys, :]
                 for half in range(2):
                     o = pair * 2 + half
-                    v = field[ys, half * N : (half + 1) * N] + bias[o]
-                    for i in range(NIN):
-                        v = v + local[i, o] * inputs[i]
+                    v = field[ys, half * N : (half + 1) * N] + pre[x, o, ys, :]
                     sq = v * v
                     t = jnp.tanh(v * (c0 + c1 * sq))
                     up = 0.5 + 0.5 * t
                     hidden = (v * up).astype(BF).astype(F32)
-                    slope[o, ys, :] = up + (0.5 * v) * (1.0 - t * t) * (c0 + (3.0 * c1) * sq)
-                    add0 = add0 + outw[o, 0] * hidden
-                    add1 = add1 + outw[o, 1] * hidden
+                    pre[x, o, ys, :] = up + (0.5 * v) * (1.0 - t * t) * (c0 + (3.0 * c1) * sq)
+                    add0 = add0 + w[half][0] * hidden
+                    add1 = add1 + w[half][1] * hidden
                 acc[0, ys, :] = add0
                 acc[1, ys, :] = add1
+
+        field_a[...] = lines(0)
+
+        @pl.loop(0, C // 4)
+        def _(turn):
+            field_b[...] = lines(turn * 2 + 1)
+            activate(field_a, turn * 2)
+            field_a[...] = lines(jnp.minimum(turn * 2 + 2, C // 2 - 1))
+            activate(field_b, turn * 2 + 1)
 
         for j in range(2):
             value = acc[j] + outb[j]
             pred[j, x] = value
             acc[j] = value - targ[j, x]
 
-        @pl.loop(0, C // 2)
-        def _(pair):
-            parts = []
-            for half in range(2):
-                o = pair * 2 + half
-                parts.append(((outw[o, 0] * acc[0] + outw[o, 1] * acc[1]) * slope[o]).astype(BF))
-            both = mm(fy[...], jnp.concatenate(parts, axis=1))
-            u = both[: 2 * K] + both[2 * K :]
-            at = pl.multiple_of(pair * 4 * N, 4 * N)
-            for half in range(2):
-                lanes = slice(half * N, (half + 1) * N)
-                ubuf[rows, pl.ds(at + 2 * half * N, N)] = u[:K, lanes]
-                ubuf[rows, pl.ds(at + (2 * half + 1) * N, N)] = u[K:, lanes]
+        @pl.loop(0, C // 8)
+        def _(turn):
+            for sub in range(4):
+                pair = turn * 4 + sub
+                parts = []
+                for half in range(2):
+                    o = pair * 2 + half
+                    grad_o = outw[0, pl.ds(o, 1), :] * acc[0] + outw[1, pl.ds(o, 1), :] * acc[1]
+                    parts.append((grad_o * pre[x, o]).astype(BF))
+                u = mm(fy[: 2 * K, :], jnp.concatenate(parts, axis=1))
+                at = pl.multiple_of(pair * 4 * N, 4 * N)
+                for half in range(2):
+                    lanes = slice(half * N, (half + 1) * N)
+                    ubuf[rows, pl.ds(at + 2 * half * N, N)] = u[:K, lanes]
+                    ubuf[rows, pl.ds(at + (2 * half + 1) * N, N)] = u[K:, lanes]
 
     for og in range(4):
-        v = left3(ubuf[:, og * 16 * N : (og + 1) * 16 * N], zg_h[...], zg_l[...])
+        high, low = split(ubuf[:, og * 16 * N : (og + 1) * 16 * N])
+        v = mm(high, zg[...]) + mm(low, zg[...])
         for x in range(planes):
             sg[:, x, og * 2 * N : (og + 1) * 2 * N] = v[x * K : (x + 1) * K, :]
 
@@ -362,15 +390,13 @@
 def body(dp, slab, consts, profiles, target_fields, lift_weight, local_weight, local_bias, output_weight, output_bias, mode_weight):
     planes = profiles.shape[2]
     share = K // dp
-    local = jnp.sum(lift_weight[:, :, None] * local_weight.astype(F32)[None], axis=1)
-    lift_wide = jnp.repeat(lift_weight, C, axis=1)
     vmem = pl.BlockSpec(memory_space=pltpu.VMEM)
     smem = pl.BlockSpec(memory_space=pltpu.SMEM)
     dma = pltpu.SemaphoreType.DMA
     pred, grad = pl.pallas_call(
         functools.partial(kernel, dp, slab),
         out_shape=(jax.ShapeDtypeStruct((2, planes, N, N), F32), jax.ShapeDtypeStruct((2, share * K, C * C), F32)),
-        in_specs=[vmem] * 4 + [smem] * 5 + [vmem] * len(consts),
+        in_specs=[vmem] * 6 + [smem] * 3 + [vmem] * len(consts),
         out_specs=(vmem, vmem),
         scratch_shapes=[
             pltpu.VMEM((planes * K, C * 2 * N), F32),
@@ -389,9 +415,11 @@
             pltpu.VMEM((slab, planes, 8 * N), F32),
             pltpu.VMEM((planes * K, 8 * N), F32),
             pltpu.VMEM((C, planes * K, 2 * N), BF),
-            pltpu.VMEM((C, planes * K, 2 * N), BF),
             pltpu.VMEM((N, 2 * N), F32),
-            pltpu.VMEM((C, N, N), F32),
+            pltpu.VMEM((N, 2 * N), F32),
+            pltpu.VMEM((planes, C, N, N), F32),
+            pltpu.VMEM((NIN, C, N), F32),
+            pltpu.VMEM((2, C, N), F32),
             pltpu.VMEM((2, N, N), F32),
             pltpu.VMEM((slab, planes, 8 * N), F32),
             pltpu.VMEM((slab, planes, 8 * N), F32),
@@ -402,8 +430,8 @@
             dma((slab,)), dma((slab,)), dma((slab,)), dma((slab,)), dma((slab,)), dma((slab,)), dma((dp,)), dma((dp,)),
         ],
         compiler_params=pltpu.CompilerParams(collective_id=0, has_side_effects=True, vmem_limit_bytes=56 << 20),
-    )(profiles[0], target_fields[0], mode_weight.reshape(2, K * K, C * C), lift_wide, lift_weight, local, local_bias,
-      output_weight.astype(F32), output_bias, *consts)
+    )(profiles[0], target_fields[0], mode_weight.reshape(2, K * K, C * C), lift_weight, local_weight,
+      output_weight.T, lift_weight, local_bias, output_bias, *consts)
     return pred[None], grad.reshape(2, 1, share, K, C * C)
 
 

time: 122 us -> 90.3 us (0.74)
  Pallas kernels: 113 us -> 86.1 us
  local copies, waits for them, and re-layouts: 6.17 us -> 3.36 us
  other arithmetic: 2.07 us -> 0 us
    pallas_call x1, Pallas kernels: 113 us -> 86.1 us  [body(): pl.pallas_call(functools.partial(kernel, dp, slab), out_shape=(jax.ShapeD...]
    reduce_sum x1 -> x0, other arithmetic: 1.37 us -> none  [body(): jnp.sum(lift_weight[:, :, None] * local_weight.astype(F32)[None], axis=1)]
    convert_element_type x1 -> x0, local copies, waits for them, and re-layouts: 1.35 us -> none  [body(): output_weight.astype(F32)]
where the time goes in v2:
time: 90.3 us; the launch traced here: 90.1 us
  Pallas kernels  86.1 us (95%)
  local copies, waits for them, and re-layouts  3.36 us (4%)
    pallas_call x1, Pallas kernels, body(): pl.pallas_call(functools.partial(kernel, dp, slab), out_shape=(jax.ShapeD...  86.1 us
    unnamed x4, local copies, waits for them, and re-layouts  3.36 us

profile of v2, /device:TPU:25, one launch (start us, length us, event | category | flops | bytes accessed | tf_op | source)
XLA Modules:
  0.0 90.1 jit_solution(15077254214344844940)
XLA Ops:
  0.6 86.1 %shard_map.221 = (f32[2,8,128,128]{3,2,1,0:T(8,128)}, f32[2,128,1024]{2,1,0:T(8,128)}) custom-call(f32[4,8,128,128]{3,2,1,0:T(8,128)} %bitcast.8, f32[2,8,128,128]{3,2,1,0:T(8,128)} %bitcast.10, f32[2,256,1024]{2,1,0:T(8,128)} %bitcast.9, f32[4,32]{1,0:T(4,128)} %lift.1, bf16[32,32]{1,0:T(8,128)(2,1)} %local.1, bf16[2,32]{1,0:T(2,128)(2,1)} %bitcast.13, ...), custom_call_target="tpu_custom_call" | custom-call | tf_op jit(solution)/shard_map/pallas_call | solution.py:396
  86.7 0.0 copy-start
  86.8 2.4 %copy.27 = f32[1,2,8,128,128]{4,3,2,1,0:T(8,128)} copy(f32[1,2,8,128,128]{4,3,2,1,0:T(8,128)} %bitcast.12) | data formatting | bytes 2097152
  89.1 0.0 copy-done
  89.1 1.0 %copy.28 = f32[2,1,8,16,1024]{4,3,2,1,0:T(8,128)} copy(f32[2,1,8,16,1024]{4,3,2,1,0:T(8,128)S(1)} %bitcast.11) | data formatting | bytes 2097152
Async XLA Ops:
  86.7 2.4 %copy-start = (f32[2,128,1024]{2,1,0:T(8,128)S(1)}, f32[2,128,1024]{2,1,0:T(8,128)}, u32[]{:S(2)}) copy-start(f32[2,128,1024]{2,1,0:T(8,128)} %get-tuple-element.5) | copy-start | bytes 3145732

commit v3 on v2

--- a/solution.py
+++ b/solution.py
@@ -96,13 +96,14 @@
 def kernel(dp, slab, prof, targ, modes, lift_rows, local, outw_rows, lift, bias, outb,
            fy, zp_h, zp_l, zg, iz, iy, fx_h, fx_l, ix_h, ix_l, rep, tile, owner, masks,
            pred, grad,
-           ubuf, resid, rows_pad, sp, rp, spec, e_h, e_l, wide, s_re, s_im, mixed, sm, rm, pm, b_h,
+           ubuf, resid, rows_pad, sp, rp, sr, rr, spec, e_h, e_l, wide, s_re, s_im, mixed, sm, rm, pm, b_h,
            field_a, field_b, pre, mix, outw, acc, sg, rg, xs, rx, g_re, g_im,
-           p_send, p_recv, m_send, m_recv, g_send, g_recv, x_send, x_recv):
+           p_send, p_recv, r_send, r_recv, m_send, m_recv, g_send, g_recv, x_send, x_recv):
     me = lax.axis_index("slab")
     mine = lax.axis_index("dp")
     planes = prof.shape[1]
     share = K // dp
+    some = planes // 2
 
     barrier = pltpu.get_barrier_semaphore()
     for step in range(1, slab):
@@ -164,6 +165,16 @@
             ubuf[rows, 2 * i * N : (2 * i + 1) * N] = u[:K]
             ubuf[rows, (2 * i + 1) * N : (2 * i + 2) * N] = u[K:]
 
+    v = left3(ubuf[:, : 2 * NIN * N], zp_h[...], zp_l[...])
+    for x in range(planes):
+        sp[:, x, :] = v[x * K : (x + 1) * K, :]
+
+    pl.semaphore_wait(barrier, slab + dp - 2)
+    pairs = copies(sp, rp, p_send, p_recv, "slab", me, slab)
+    launch(pairs, sp, rp, me)
+
+    @pl.loop(0, planes)
+    def _(x):
         @pl.loop(0, C // 4)
         def _(group):
             totals = [resid[group * 4 + j] for j in range(4)]
@@ -180,9 +191,6 @@
             for j in range(4):
                 resid[group * 4 + j] = totals[j]
 
-    v = left3(ubuf[:, : 2 * NIN * N], zp_h[...], zp_l[...])
-    for x in range(planes):
-        sp[:, x, :N] = v[x * K : (x + 1) * K, :]
     rows_pad[...] = jnp.zeros_like(rows_pad)
     rows_pad[N // 2 : N // 2 + C, :] = jnp.sum(resid[...], axis=1)
     high, low = split(rows_pad[...])
@@ -191,19 +199,14 @@
     sums = lax.dot_general(ones, high, dims, preferred_element_type=F32)
     sums = sums + lax.dot_general(ones, low, dims, preferred_element_type=F32)
     for q in range(slab):
-        sp[q, :, N:] = sums
-
-    pl.semaphore_wait(barrier, slab + dp - 2)
-    pairs = copies(sp, rp, p_send, p_recv, "slab", me, slab)
-    launch(pairs, sp, rp, me)
+        sr[q] = sums
+    more = copies(sr, rr, r_send, r_recv, "slab", me, slab)
+    launch(more, sr, rr, me)
     finish(pairs)
 
-    y = right3(fx_h[...], fx_l[...], rp[:, :, :N].reshape(N, N))
+    y = right3(fx_h[...], fx_l[...], rp[...].reshape(N, N))
     spec[:, :N] = y[:K] + masks[4] * pltpu.roll(y[K:], N // 2, 1)
-    sums = jnp.sum(rp[:, :, N:].reshape(N, N), axis=0, keepdims=True)
-    scale = jnp.where(me == 0, 1.0 / (planes * math.sqrt(N * N * N)), 0.0).astype(F32)
     spec[:, N:] = jnp.zeros((K, N), F32)
-    spec[:1, N:] = sums * scale
 
     def expand(row_of, count):
         for p in range(count):
@@ -231,6 +234,20 @@
             value = value + pltpu.roll(value, 64, 1)
             mixed[part, rows, :] = value + pltpu.roll(value, 32, 1)
 
+    finish(more)
+    sums = jnp.sum(rr[...].reshape(N, N), axis=0, keepdims=True)
+    scale = jnp.where(me == 0, 1.0 / (planes * math.sqrt(N * N * N)), 0.0).astype(F32)
+    spec[:1, N:] = sums * scale
+    high, low = split(jnp.broadcast_to(sums * scale, (K, N)))
+    lost = (mm(high, owner[...]) + mm(low, owner[...]))[:1, :]
+    for part in range(2):
+        value = jnp.zeros((1, N), F32)
+        for t in range(C * C // N):
+            lanes = slice(t * N, (t + 1) * N)
+            value = value + lost[:, lanes] * modes[part, :1, lanes]
+        value = value + pltpu.roll(value, 64, 1)
+        mixed[part, :1, :] += value + pltpu.roll(value, 32, 1)
+
     spread = []
     for part in range(2):
         high, low = split(mixed[part])
@@ -241,11 +258,19 @@
         re, im = spread[0][:, lanes] * keep, spread[1][:, lanes] * keep
         out_re = right3(ix_h[0], ix_l[0], re) - right3(ix_h[1], ix_l[1], im)
         out_im = right3(ix_h[0], ix_l[0], im) + right3(ix_h[1], ix_l[1], re)
-        sm[:, :, 2 * og * N : (2 * og + 1) * N] = out_re.reshape(slab, planes, N)
-        sm[:, :, (2 * og + 1) * N : (2 * og + 2) * N] = out_im.reshape(slab, planes, N)
-
-    pairs = copies(sm, rm, m_send, m_recv, "slab", me, slab)
-    launch(pairs, sm, rm, me)
+        for h in range(2):
+            for d in range(slab):
+                first = d * planes + h * some
+                sm[h, d, :, 2 * og * N : (2 * og + 1) * N] = out_re[first : first + some]
+        for h in range(2):
+            for d in range(slab):
+                first = d * planes + h * some
+                sm[h, d, :, (2 * og + 1) * N : (2 * og + 2) * N] = out_im[first : first + some]
+
+    moving = []
+    for h in range(2):
+        moving.append(copies(sm.at[h], rm.at[h], m_send.at[h], m_recv.at[h], "slab", me, slab))
+        launch(moving[h], sm.at[h], rm.at[h], me)
 
     @pl.loop(0, planes)
     def _(x):
@@ -261,89 +286,100 @@
                         value = value + mix[i, pl.ds(o, 1), :] * inputs[i]
                     pre[x, o, ys, :] = value
 
-    finish(pairs)
-
-    for x in range(planes):
-        pm[x * K : (x + 1) * K, :] = rm[:, x, :]
-    for og in range(4):
-        high = pm[:, og * 2 * N : (og + 1) * 2 * N].astype(BF)
-        for t in range(8):
-            b_h[og * 8 + t] = mm(high, iz[:, t * 2 * N : (t + 1) * 2 * N]).astype(BF)
-
     c0 = math.sqrt(2.0 / math.pi)
     c1 = c0 * 0.044715
 
-    @pl.loop(0, planes)
-    def _(x):
-        rows = pl.ds(pl.multiple_of(x * K, K), K)
-        acc[...] = jnp.zeros_like(acc)
-
-        def lines(pair):
-            blocks = []
-            for half in range(2):
-                b = b_h[pair * 2 + half, rows, :]
-                blocks.append(jnp.concatenate([b[:, :N], b[:, N:]], axis=0))
-            return mm(iy[...], jnp.concatenate(blocks, axis=1))
-
-        def activate(field, pair):
-            w = [[outw[j, pl.ds(pair * 2 + half, 1), :] for j in range(2)] for half in range(2)]
-            for chunk in range(4):
-                ys = slice(chunk * 32, (chunk + 1) * 32)
-                add0, add1 = acc[0, ys, :], acc[1, ys, :]
+    leaving = []
+
+    def half_planes(h):
+        finish(moving[h])
+        top = h * some * K
+        bottom = top + some * K
+        for x in range(some):
+            pm[top + x * K : top + (x + 1) * K, :] = rm[h, :, x, :]
+        for og in range(4):
+            high = pm[top:bottom, og * 2 * N : (og + 1) * 2 * N].astype(BF)
+            for t in range(8):
+                b_h[og * 8 + t, top:bottom, :] = mm(high, iz[:, t * 2 * N : (t + 1) * 2 * N]).astype(BF)
+
+        @pl.loop(h * some, (h + 1) * some)
+        def _(x):
+            rows = pl.ds(pl.multiple_of(x * K, K), K)
+            acc[...] = jnp.zeros_like(acc)
+
+            def lines(pair):
+                blocks = []
                 for half in range(2):
-                    o = pair * 2 + half
-                    v = field[ys, half * N : (half + 1) * N] + pre[x, o, ys, :]
-                    sq = v * v
-                    t = jnp.tanh(v * (c0 + c1 * sq))
-                    up = 0.5 + 0.5 * t
-                    hidden = (v * up).astype(BF).astype(F32)
-                    pre[x, o, ys, :] = up + (0.5 * v) * (1.0 - t * t) * (c0 + (3.0 * c1) * sq)
-                    add0 = add0 + w[half][0] * hidden
-                    add1 = add1 + w[half][1] * hidden
-                acc[0, ys, :] = add0
-                acc[1, ys, :] = add1
-
-        field_a[...] = lines(0)
-
-        @pl.loop(0, C // 4)
-        def _(turn):
-            field_b[...] = lines(turn * 2 + 1)
-            activate(field_a, turn * 2)
-            field_a[...] = lines(jnp.minimum(turn * 2 + 2, C // 2 - 1))
-            activate(field_b, turn * 2 + 1)
-
-        for j in range(2):
-            value = acc[j] + outb[j]
-            pred[j, x] = value
-            acc[j] = value - targ[j, x]
-
-        @pl.loop(0, C // 8)
-        def _(turn):
-            for sub in range(4):
-                pair = turn * 4 + sub
-                parts = []
-                for half in range(2):
-                    o = pair * 2 + half
-                    grad_o = outw[0, pl.ds(o, 1), :] * acc[0] + outw[1, pl.ds(o, 1), :] * acc[1]
-                    parts.append((grad_o * pre[x, o]).astype(BF))
-                u = mm(fy[: 2 * K, :], jnp.concatenate(parts, axis=1))
-                at = pl.multiple_of(pair * 4 * N, 4 * N)
-                for half in range(2):
-                    lanes = slice(half * N, (half + 1) * N)
-                    ubuf[rows, pl.ds(at + 2 * half * N, N)] = u[:K, lanes]
-                    ubuf[rows, pl.ds(at + (2 * half + 1) * N, N)] = u[K:, lanes]
-
-    for og in range(4):
-        high, low = split(ubuf[:, og * 16 * N : (og + 1) * 16 * N])
-        v = mm(high, zg[...]) + mm(low, zg[...])
-        for x in range(planes):
-            sg[:, x, og * 2 * N : (og + 1) * 2 * N] = v[x * K : (x + 1) * K, :]
-
-    pairs = copies(sg, rg, g_send, g_recv, "slab", me, slab)
-    launch(pairs, sg, rg, me)
-    finish(pairs)
-
-    y = right3(fx_h[...], fx_l[...], rg[...].reshape(N, 8 * N))
+                    b = b_h[pair * 2 + half, rows, :]
+                    blocks.append(jnp.concatenate([b[:, :N], b[:, N:]], axis=0))
+                return mm(iy[...], jnp.concatenate(blocks, axis=1))
+
+            def activate(field, pair):
+                w = [[outw[j, pl.ds(pair * 2 + half, 1), :] for j in range(2)] for half in range(2)]
+                for chunk in range(4):
+                    ys = slice(chunk * 32, (chunk + 1) * 32)
+                    add0, add1 = acc[0, ys, :], acc[1, ys, :]
+                    for half in range(2):
+                        o = pair * 2 + half
+                        v = field[ys, half * N : (half + 1) * N] + pre[x, o, ys, :]
+                        sq = v * v
+                        t = jnp.tanh(v * (c0 + c1 * sq))
+                        up = 0.5 + 0.5 * t
+                        hidden = (v * up).astype(BF).astype(F32)
+                        pre[x, o, ys, :] = up + (0.5 * v) * (1.0 - t * t) * (c0 + (3.0 * c1) * sq)
+                        add0 = add0 + w[half][0] * hidden
+                        add1 = add1 + w[half][1] * hidden
+                    acc[0, ys, :] = add0
+                    acc[1, ys, :] = add1
+
+            field_a[...] = lines(0)
+
+            @pl.loop(0, C // 4)
+            def _(turn):
+                field_b[...] = lines(turn * 2 + 1)
+                activate(field_a, turn * 2)
+                field_a[...] = lines(jnp.minimum(turn * 2 + 2, C // 2 - 1))
+                activate(field_b, turn * 2 + 1)
+
+            for j in range(2):
+                value = acc[j] + outb[j]
+                pred[j, x] = value
+                acc[j] = value - targ[j, x]
+
+            @pl.loop(0, C // 8)
+            def _(turn):
+                for sub in range(4):
+                    pair = turn * 4 + sub
+                    parts = []
+                    for half in range(2):
+                        o = pair * 2 + half
+                        grad_o = outw[0, pl.ds(o, 1), :] * acc[0] + outw[1, pl.ds(o, 1), :] * acc[1]
+                        parts.append((grad_o * pre[x, o]).astype(BF))
+                    u = mm(fy[: 2 * K, :], jnp.concatenate(parts, axis=1))
+                    at = pl.multiple_of(pair * 4 * N, 4 * N)
+                    for half in range(2):
+                        lanes = slice(half * N, (half + 1) * N)
+                        ubuf[rows, pl.ds(at + 2 * half * N, N)] = u[:K, lanes]
+                        ubuf[rows, pl.ds(at + (2 * half + 1) * N, N)] = u[K:, lanes]
+
+        for og in range(4):
+            high, low = split(ubuf[top:bottom, og * 16 * N : (og + 1) * 16 * N])
+            v = mm(high, zg[...]) + mm(low, zg[...])
+            for x in range(some):
+                sg[h, :, x, og * 2 * N : (og + 1) * 2 * N] = v[x * K : (x + 1) * K, :]
+
+        leaving.append(copies(sg.at[h], rg.at[h], g_send.at[h], g_recv.at[h], "slab", me, slab))
+        launch(leaving[h], sg.at[h], rg.at[h], me)
+
+    half_planes(0)
+    half_planes(1)
+    for h in range(2):
+        finish(leaving[h])
+        for d in range(slab):
+            first = d * planes + h * some
+            pm[first : first + some, :] = rg[h, d]
+
+    y = right3(fx_h[...], fx_l[...], pm[...])
     for og in range(4):
         re, im = slice(2 * og * N, (2 * og + 1) * N), slice((2 * og + 1) * N, (2 * og + 2) * N)
         out_re = (y[:K, re] - y[K:, im]) * masks[3]
@@ -402,8 +438,10 @@
             pltpu.VMEM((planes * K, C * 2 * N), F32),
             pltpu.VMEM((C, 8, N), F32),
             pltpu.VMEM((N, N), F32),
-            pltpu.VMEM((slab, planes, 2 * N), F32),
-            pltpu.VMEM((slab, planes, 2 * N), F32),
+            pltpu.VMEM((slab, planes, N), F32),
+            pltpu.VMEM((slab, planes, N), F32),
+            pltpu.VMEM((slab, planes, N), F32),
+            pltpu.VMEM((slab, planes, N), F32),
             pltpu.VMEM((K, 2 * N), F32),
             pltpu.VMEM((N, C * C), BF),
             pltpu.VMEM((N, C * C), BF),
@@ -411,8 +449,8 @@
             pltpu.VMEM((K * K, C * C), F32),
             pltpu.VMEM((K * K, C * C), F32),
             pltpu.VMEM((2, K * K, N), F32),
-            pltpu.VMEM((slab, planes, 8 * N), F32),
-            pltpu.VMEM((slab, planes, 8 * N), F32),
+            pltpu.VMEM((2, slab, planes // 2, 8 * N), F32),
+            pltpu.VMEM((2, slab, planes // 2, 8 * N), F32),
             pltpu.VMEM((planes * K, 8 * N), F32),
             pltpu.VMEM((C, planes * K, 2 * N), BF),
             pltpu.VMEM((N, 2 * N), F32),
@@ -421,13 +459,14 @@
             pltpu.VMEM((NIN, C, N), F32),
             pltpu.VMEM((2, C, N), F32),
             pltpu.VMEM((2, N, N), F32),
-            pltpu.VMEM((slab, planes, 8 * N), F32),
-            pltpu.VMEM((slab, planes, 8 * N), F32),
+            pltpu.VMEM((2, slab, planes // 2, 8 * N), F32),
+            pltpu.VMEM((2, slab, planes // 2, 8 * N), F32),
             pltpu.VMEM((dp, share, 10 * N), F32),
             pltpu.VMEM((dp, share, 10 * N), F32),
             pltpu.VMEM((share * K, N), F32),
             pltpu.VMEM((share * K, N), F32),
-            dma((slab,)), dma((slab,)), dma((slab,)), dma((slab,)), dma((slab,)), dma((slab,)), dma((dp,)), dma((dp,)),
+            dma((slab,)), dma((slab,)), dma((slab,)), dma((slab,)),
+            dma((2, slab)), dma((2, slab)), dma((2, slab)), dma((2, slab)), dma((dp,)), dma((dp,)),
         ],
         compiler_params=pltpu.CompilerParams(collective_id=0, has_side_effects=True, vmem_limit_bytes=56 << 20),
     )(profiles[0], target_fields[0], mode_weight.reshape(2, K * K, C * C), lift_weight, local_weight,

time: 90.3 us -> 81.8 us (0.906)
  the two profiles are of different devices: /device:TPU:25 before, /device:TPU:0 now
where the time goes in v3:
time: 81.8 us; the launch traced here: 81.7 us
  Pallas kernels  77.7 us (95%)
  local copies, waits for them, and re-layouts  3.36 us (4%)
    pallas_call x1, Pallas kernels, body(): pl.pallas_call(functools.partial(kernel, dp, slab), out_shape=(jax.ShapeD...  77.7 us
    unnamed x4, local copies, waits for them, and re-layouts  3.36 us

profile of v3, /device:TPU:0, one launch (start us, length us, event | category | flops | bytes accessed | tf_op | source)
XLA Modules:
  0.0 81.7 jit_solution(3624855056144037912)
XLA Ops:
  0.6 77.7 %shard_map.221 = (f32[2,8,128,128]{3,2,1,0:T(8,128)}, f32[2,128,1024]{2,1,0:T(8,128)}) custom-call(f32[4,8,128,128]{3,2,1,0:T(8,128)} %bitcast.8, f32[2,8,128,128]{3,2,1,0:T(8,128)} %bitcast.10, f32[2,256,1024]{2,1,0:T(8,128)} %bitcast.9, f32[4,32]{1,0:T(4,128)} %lift.1, bf16[32,32]{1,0:T(8,128)(2,1)} %local.1, bf16[2,32]{1,0:T(2,128)(2,1)} %bitcast.13, ...), custom_call_target="tpu_custom_call" | custom-call | tf_op jit(solution)/shard_map/pallas_call | solution.py:432
  78.3 0.0 copy-start
  78.3 2.4 %copy.27 = f32[1,2,8,128,128]{4,3,2,1,0:T(8,128)} copy(f32[1,2,8,128,128]{4,3,2,1,0:T(8,128)} %bitcast.12) | data formatting | bytes 2097152
  80.7 0.0 copy-done
  80.7 1.0 %copy.28 = f32[2,1,8,16,1024]{4,3,2,1,0:T(8,128)} copy(f32[2,1,8,16,1024]{4,3,2,1,0:T(8,128)S(1)} %bitcast.11) | data formatting | bytes 2097152
Async XLA Ops:
  78.3 2.4 %copy-start = (f32[2,128,1024]{2,1,0:T(8,128)S(1)}, f32[2,128,1024]{2,1,0:T(8,128)}, u32[]{:S(2)}) copy-start(f32[2,128,1024]{2,1,0:T(8,128)} %get-tuple-element.5) | copy-start | bytes 3145732
